TPU v7x, 32 devices: a whole 2x2x4 slice. The times are simulated.
32 devices in a mesh: ctx: 8 (over y, x, core), head: 4 (over z).
Axes of the slice: x: 2, y: 2, z: 4, core: 2. Of those that a mesh axis runs over, the one named last changes fastest.
Arguments:
- queries: bfloat16 [4096, 4096], P('ctx', 'head'), may hold values from -8 to 8
- keys: bfloat16 [4096, 1024], P('ctx', 'head'), may hold values from -8 to 8
- values: bfloat16 [4096, 1024], P('ctx', 'head'), may hold values from -6 to 6
- lengths: int32 [16], replicated, may hold values from 1 to 1024, 4096 in all
- out_weight: bfloat16 [4096, 4096], P(None, 'head'), may hold values from -0.09375 to 0.09375
Outputs:
- mixed: bfloat16 [4096, 4096], P('ctx', 'head')
Inputs may be any that keep to these rules, and one draw needn't show every extreme that they name: `lengths`: each document holds at least one token and one holds exactly 1024; they sum to 4096.
All inputs are finite; a program needn't handle non-finite values.
Results may differ from a plain program's by a relative error of at most 0.0085.
Values may be sent and summed in bfloat16 or wider, within the bound.
No kernel may reach another device: no remote copies, remote signals or barrier semaphores. Data moves between devices by JAX's collectives and lax.ppermute only.
A program may use at most 64 MiB of HBM per device.

v0:
```python
import jax
import jax.numpy as jnp
from jax import lax
from jax.sharding import PartitionSpec as P

HEAD_SIZE = 128


def shifted(shard, axis, by):
    peers = lax.axis_size(axis)
    pairs = [(i, i + by) for i in range(peers) if 0 <= i + by < peers]
    return lax.ppermute(shard, axis, pairs)


def doc_labels(lengths, positions):
    boundary = jnp.cumsum(lengths)
    return jnp.sum((boundary[None, :] <= positions[:, None]).astype(jnp.int32), axis=1) + 1


def attend(softmax_state, grouped_queries, labels, key_block, value_block, key_labels, causal):
    tok_local = grouped_queries.shape[0]
    kv_local = key_block.shape[1] // HEAD_SIZE
    keyed_rows = key_block.reshape(tok_local, kv_local, HEAD_SIZE)
    valued_rows = value_block.reshape(tok_local, kv_local, HEAD_SIZE)
    scores = jnp.einsum(
        "tkgd,skd->kgts", grouped_queries, keyed_rows, preferred_element_type=jnp.float32
    ) * HEAD_SIZE ** (-0.5)
    allowed = labels[:, None] == key_labels[None, :]
    if causal:
        allowed = allowed & jnp.tril(jnp.ones((tok_local, tok_local), dtype=bool))
    scores = jnp.where(allowed, scores, -1e30)
    run_max, run_total, numer = softmax_state
    new_max = jnp.maximum(run_max, jnp.max(scores, axis=-1))
    factor = jnp.exp(run_max - new_max)
    weights = jnp.exp(scores - new_max[..., None])
    run_total = run_total * factor + jnp.sum(weights, axis=-1)
    numer = numer * factor[..., None] + jnp.einsum(
        "kgts,skd->kgtd",
        weights.astype(jnp.bfloat16),
        valued_rows,
        preferred_element_type=jnp.float32,
    )
    return (new_max, run_total, numer)


def shards(queries, keys, values, lengths, out_weight):
    tok_local = queries.shape[0]
    kv_local = keys.shape[1] // HEAD_SIZE
    query_group_size = queries.shape[1] // keys.shape[1]
    positions = lax.axis_index("ctx") * tok_local + jnp.arange(tok_local, dtype=jnp.int32)
    labels = doc_labels(lengths, positions)
    grouped_queries = queries.reshape(tok_local, kv_local, query_group_size, HEAD_SIZE)
    softmax_state = (
        jnp.full((kv_local, query_group_size, tok_local), -1e30, jnp.float32),
        jnp.zeros((kv_local, query_group_size, tok_local), jnp.float32),
        jnp.zeros((kv_local, query_group_size, tok_local, HEAD_SIZE), jnp.float32),
    )
    softmax_state = attend(softmax_state, grouped_queries, labels, keys, values, labels, True)
    reach_shards = lax.axis_size("ctx") // 4

    def visit(state_now, carried):
        return (
            attend(state_now, grouped_queries, labels, carried[0], carried[1], carried[2], False),
            None,
        )

    def turn_step(turn_index, carry):
        state_now, carried = carry
        carried = shifted((carried[0], carried[1], carried[2]), "ctx", 1)
        return (visit(state_now, carried)[0], carried)

    softmax_state, unused = lax.fori_loop(
        0, reach_shards, turn_step, (softmax_state, (keys, values, labels))
    )
    run_max, run_total, numer = softmax_state
    attended = numer / run_total[..., None]
    attended = (
        jnp.transpose(attended, (2, 0, 1, 3))
        .reshape(tok_local, queries.shape[1])
        .astype(jnp.bfloat16)
    )
    mixed = jnp.dot(
        lax.all_gather(attended, "head", axis=1, tiled=True),
        out_weight,
        preferred_element_type=jnp.float32,
    )
    return mixed.astype(jnp.bfloat16)


def solution(mesh):
    return jax.shard_map(
        shards,
        mesh=mesh,
        in_specs=(P("ctx", "head"), P("ctx", "head"), P("ctx", "head"), P(), P(None, "head")),
        out_specs=P("ctx", "head"),
        check_vma=False,
    )
```

profile of v0, /device:TPU:0, one launch (start us, length us, event | category | flops | bytes accessed | tf_op | source)
XLA Modules:
  0.0 160.9 jit_solution(7699841117121816501)
XLA Ops:
  6.5 0.7 copy.27
  7.5 0.2 fusion.19
  7.7 1.0 reshape.65
  8.8 1.1 copy.33
  9.9 1.0 reshape.67
  10.9 1.1 copy.34
  12.0 1.5 copy.28
  13.5 0.7 copy.35
  14.2 1.6 fusion.12
  15.8 1.7 %fusion.11 = f32[2,4,512]{2,1,0:T(4,128)S(1)} fusion(f32[2,512,512,4]{2,1,3,0:T(8,128)S(1)} %get-tuple-element.98, f32[2,4,512]{2,1,0:T(4,128)S(1)} %broadcast_maximum_fusion, pred[512,512]{0,1:T(8,128)(4,1)S(1)} %fusion.19), kind=kLoop, calls=%fused_computation.16 | loop fusion | flops 8384512 | bytes 8683520 | tf_op jit(solution)/shard_map/reduce_sum | solution.py:36
  17.5 3.9 %fusion.16 = f32[2,4,512,128]{3,2,1,0:T(8,128)} fusion(f32[2,512,512,4]{2,1,3,0:T(8,128)S(1)} %get-tuple-element.98, f32[2,4,512]{2,1,0:T(4,128)S(1)} %broadcast_maximum_fusion, pred[512,512]{0,1:T(8,128)(4,1)S(1)} %fusion.19, f32[2,4,512]{2,1,0:T(4,128)S(1)} %get-tuple-element.95, bf16[512,2,128,1]{2,1,0,3:T(2,128)(2,1)S(1)} %bitcast.91), kind=kOutput, calls=%fused_computation.21 | convolution fusion | flops 545783808 | bytes 11042816 | tf_op jit(solution)/shard_map/kgts,skd->kgtd/dot_general | solution.py:37
  21.4 35.6 %while.20 = (s32[]{:T(128)}, f32[2,4,512]{2,1,0:T(4,128)S(1)}, f32[2,4,512]{2,1,0:T(4,128)S(1)}, f32[2,4,512,128]{3,2,1,0:T(8,128)}, bf16[512,256]{0,1:T(8,128)(...) while((s32[]{:T(128)}, f32[2,4,512]{2,1,0:T(4,128)S(1)}, ...), condition=%wide.region_7.8_spmd, body=%wide.region_4.7_spmd.sunk | while | flops 1098129408 | bytes 52183316 | solution.py:72
  21.4 2.4 %collective-permute-start.1 = (bf16[512,256]{0,1:T(8,128)(2,1)S(1)}, bf16[512,256]{0,1:T(8,128)(2,1)S(1)}, u32[]{:S(2)}, u32[]{:S(2)}) collective-permute-start(bf16[512,256]{0,1:T(8,128)(2,1)S(1)} %get-tuple-element.180), channel_id=1, source_target_pairs={{0,4},{4,8},{8,12},{12,16},{16,20},{20,24},{24,28},{1,5},{5,9},{9,... | collective-permute-start | bytes 786440 | tf_op jit(solution)/shard_map/while/body/eval_jaxpr/ppermute | solution.py:12
  23.8 4.5 %collective-permute-start = (s32[512]{0:T(512)S(1)}, s32[512]{0:T(512)S(1)}, u32[]{:S(2)}, u32[]{:S(2)}) collective-permute-start(s32[512]{0:T(512)S(1)} %get-tuple-element.182), channel_id=1, source_target_pairs={{0,4},{4,8},{8,12},{12,16},{16,20},{20,24},{24,28},{1,5},{5,9},{9,... | collective-permute-start | bytes 6152 | tf_op jit(solution)/shard_map/while/body/eval_jaxpr/ppermute | solution.py:12
  28.3 1.9 %collective-permute-start.2 = (bf16[512,256]{0,1:T(8,128)(2,1)S(1)}, bf16[512,256]{0,1:T(8,128)(2,1)S(1)}, u32[]{:S(2)}, u32[]{:S(2)}) collective-permute-start(bf16[512,256]{0,1:T(8,128)(2,1)S(1)} %get-tuple-element.181), channel_id=1, source_target_pairs={{0,4},{4,8},{8,12},{12,16},{16,20},{20,24},{24,28},{1,5},{5,9},{9,... | collective-permute-start | bytes 786440 | tf_op jit(solution)/shard_map/while/body/eval_jaxpr/ppermute | solution.py:12
  30.3 0.2 broadcast_compare_fusion.2
  30.5 2.0 %fusion.42 = (f32[2,4,512]{2,1,0:T(4,128)S(1)}, f32[2,512,512,4]{2,1,3,0:T(8,128)S(1)}) fusion(pred[512,512]{0,1:T(8,128)(4,1)S(1)} %broadcast_compare_fusion.2, bf16[512,2,128,1]{0,2,3,1:T(8,128)(2,1)S(1)} %bitcast.79, bf16[512,2,4,128]{3,0,2,1:T(8,128)(2,1)S(1)} %get-tuple-element.194), kind=kOutput, calls=%fused_computation.4.clone.1 | convolution fusion | flops 543158272 | bytes 9977856 | tf_op jit(solution)/shard_map/while/body/eval_jaxpr/tkgd,skd->kgts/dot_general | solution.py:25
  32.6 1.7 %fusion.43 = f32[2,4,512]{2,1,0:T(4,128)S(1)} fusion(f32[2,512,512,4]{2,1,3,0:T(8,128)S(1)} %get-tuple-element.163, f32[2,4,512]{2,1,0:T(4,128)S(1)} %max.4, pred[512,512]{0,1:T(8,128)(4,1)S(1)} %broadcast_compare_fusion.2), kind=kLoop, calls=%fused_computation.3.clone.1 | loop fusion | flops 8384512 | bytes 8683520 | tf_op jit(solution)/shard_map/while/body/eval_jaxpr/reduce_sum | solution.py:36
  34.4 3.4 %multiply_add_fusion.5 = f32[2,4,512,128]{3,2,1,0:T(8,128)S(1)} fusion(f32[2,4,512,128]{3,2,1,0:T(8,128)S(1)} %copy-done, bf16[512,2,128,1]{0,2,3,1:T(8,128)(2,1)S(1)} %bitcast.83, f32[2,512,512,4]{2,1,3,0:T(8,128)S(1)} %get-tuple-element.163, f32[2,4,512]{2,1,0:T(4,128)S(1)} %max.4, pred[512,512]{0,1:T(8,128)(4,1)S(1)} %broadcast_compare_fusion.2, ...), kind=kOutput, calls=%fused_computation.7.clone.1 | convolution fusion | flops 546308096 | bytes 13139968 | tf_op jit(solution)/shard_map/while/body/eval_jaxpr/kgts,skd->kgtd/dot_general | solution.py:37
  37.8 1.3 copy-done.1
  39.1 3.5 %collective-permute-start.1 = (bf16[512,256]{0,1:T(8,128)(2,1)S(1)}, bf16[512,256]{0,1:T(8,128)(2,1)S(1)}, u32[]{:S(2)}, u32[]{:S(2)}) collective-permute-start(bf16[512,256]{0,1:T(8,128)(2,1)S(1)} %get-tuple-element.180), channel_id=1, source_target_pairs={{0,4},{4,8},{8,12},{12,16},{16,20},{20,24},{24,28},{1,5},{5,9},{9,... | collective-permute-start | bytes 786440 | tf_op jit(solution)/shard_map/while/body/eval_jaxpr/ppermute | solution.py:12
  42.6 3.5 %collective-permute-start = (s32[512]{0:T(512)S(1)}, s32[512]{0:T(512)S(1)}, u32[]{:S(2)}, u32[]{:S(2)}) collective-permute-start(s32[512]{0:T(512)S(1)} %get-tuple-element.182), channel_id=1, source_target_pairs={{0,4},{4,8},{8,12},{12,16},{16,20},{20,24},{24,28},{1,5},{5,9},{9,... | collective-permute-start | bytes 6152 | tf_op jit(solution)/shard_map/while/body/eval_jaxpr/ppermute | solution.py:12
  46.2 1.9 %collective-permute-start.2 = (bf16[512,256]{0,1:T(8,128)(2,1)S(1)}, bf16[512,256]{0,1:T(8,128)(2,1)S(1)}, u32[]{:S(2)}, u32[]{:S(2)}) collective-permute-start(bf16[512,256]{0,1:T(8,128)(2,1)S(1)} %get-tuple-element.181), channel_id=1, source_target_pairs={{0,4},{4,8},{8,12},{12,16},{16,20},{20,24},{24,28},{1,5},{5,9},{9,... | collective-permute-start | bytes 786440 | tf_op jit(solution)/shard_map/while/body/eval_jaxpr/ppermute | solution.py:12
  48.1 0.2 broadcast_compare_fusion.2
  48.4 2.0 %fusion.42 = (f32[2,4,512]{2,1,0:T(4,128)S(1)}, f32[2,512,512,4]{2,1,3,0:T(8,128)S(1)}) fusion(pred[512,512]{0,1:T(8,128)(4,1)S(1)} %broadcast_compare_fusion.2, bf16[512,2,128,1]{0,2,3,1:T(8,128)(2,1)S(1)} %bitcast.79, bf16[512,2,4,128]{3,0,2,1:T(8,128)(2,1)S(1)} %get-tuple-element.194), kind=kOutput, calls=%fused_computation.4.clone.1 | convolution fusion | flops 543158272 | bytes 9977856 | tf_op jit(solution)/shard_map/while/body/eval_jaxpr/tkgd,skd->kgts/dot_general | solution.py:25
  50.4 1.7 %fusion.43 = f32[2,4,512]{2,1,0:T(4,128)S(1)} fusion(f32[2,512,512,4]{2,1,3,0:T(8,128)S(1)} %get-tuple-element.163, f32[2,4,512]{2,1,0:T(4,128)S(1)} %max.4, pred[512,512]{0,1:T(8,128)(4,1)S(1)} %broadcast_compare_fusion.2), kind=kLoop, calls=%fused_computation.3.clone.1 | loop fusion | flops 8384512 | bytes 8683520 | tf_op jit(solution)/shard_map/while/body/eval_jaxpr/reduce_sum | solution.py:36
  52.2 3.4 %multiply_add_fusion.5 = f32[2,4,512,128]{3,2,1,0:T(8,128)S(1)} fusion(f32[2,4,512,128]{3,2,1,0:T(8,128)S(1)} %copy-done, bf16[512,2,128,1]{0,2,3,1:T(8,128)(2,1)S(1)} %bitcast.83, f32[2,512,512,4]{2,1,3,0:T(8,128)S(1)} %get-tuple-element.163, f32[2,4,512]{2,1,0:T(4,128)S(1)} %max.4, pred[512,512]{0,1:T(8,128)(4,1)S(1)} %broadcast_compare_fusion.2, ...), kind=kOutput, calls=%fused_computation.7.clone.1 | convolution fusion | flops 546308096 | bytes 13139968 | tf_op jit(solution)/shard_map/while/body/eval_jaxpr/kgts,skd->kgtd/dot_general | solution.py:37
  55.7 1.3 copy-done.1
  57.0 1.9 %copy.36 = f32[2,4,512,128]{2,3,1,0:T(8,128)S(1)} copy(f32[2,4,512,128]{3,2,1,0:T(8,128)} %get-tuple-element.53) | data formatting | bytes 4194304 | tf_op jit(solution)/shard_map/while | solution.py:72
  58.9 1.2 divide_convert_fusion
  60.2 83.7 %all-gather.2.cloned.1.call-done = bf16[512,4096]{0,1:T(8,128)(2,1)} async-done(((bf16[512,1024]{0,1:T(8,128)(2,1)}), bf16[512,4096]{0,1:T(8,128)(2,1)}) %all-gather.2.cloned.1.call-update) | async-done | bytes 4194320 | tf_op jit(solution)/shard_map/all_gather | solution.py:83
  143.9 10.1 %convolution_convert_fusion = bf16[512,1024]{1,0:T(8,128)(2,1)} fusion(bf16[512,4096]{0,1:T(8,128)(2,1)} %all-gather.2.cloned.1.call-done, bf16[4096,1024]{1,0:T(8,128)(2,1)} %param.11), kind=kOutput, calls=%fused_computation.22 | convolution fusion | flops 4295491584 | bytes 13631488 | tf_op jit(solution)/shard_map/dot_general | solution.py:82
  (34 shorter events, 0.5 us)
Async XLA Ops:
  6.5 137.4 %all-gather.2.cloned.1.call-start = ((), (), s32[]{:S(2)}) async-start(), calls=%async_computation | async-start | bytes 5242880 | tf_op jit(solution)/shard_map/all_gather | solution.py:83
  21.4 9.1 %collective-permute-start.1 = (bf16[512,256]{0,1:T(8,128)(2,1)S(1)}, bf16[512,256]{0,1:T(8,128)(2,1)S(1)}, u32[]{:S(2)}, u32[]{:S(2)}) collective-permute-start(bf16[512,256]{0,1:T(8,128)(2,1)S(1)} %get-tuple-element.180), channel_id=1, source_target_pairs={{0,4},{4,8},{8,12},{12,16},{16,20},{20,24},{24,28},{1,5},{5,9},{9,... | collective-permute-start | bytes 786440 | tf_op jit(solution)/shard_map/while/body/eval_jaxpr/ppermute | solution.py:12
  23.8 6.4 %collective-permute-start = (s32[512]{0:T(512)S(1)}, s32[512]{0:T(512)S(1)}, u32[]{:S(2)}, u32[]{:S(2)}) collective-permute-start(s32[512]{0:T(512)S(1)} %get-tuple-element.182), channel_id=1, source_target_pairs={{0,4},{4,8},{8,12},{12,16},{16,20},{20,24},{24,28},{1,5},{5,9},{9,... | collective-permute-start | bytes 6152 | tf_op jit(solution)/shard_map/while/body/eval_jaxpr/ppermute | solution.py:12
  28.3 6.0 %collective-permute-start.2 = (bf16[512,256]{0,1:T(8,128)(2,1)S(1)}, bf16[512,256]{0,1:T(8,128)(2,1)S(1)}, u32[]{:S(2)}, u32[]{:S(2)}) collective-permute-start(bf16[512,256]{0,1:T(8,128)(2,1)S(1)} %get-tuple-element.181), channel_id=1, source_target_pairs={{0,4},{4,8},{8,12},{12,16},{16,20},{20,24},{24,28},{1,5},{5,9},{9,... | collective-permute-start | bytes 786440 | tf_op jit(solution)/shard_map/while/body/eval_jaxpr/ppermute | solution.py:12
  30.5 3.9 %copy-start = (f32[2,4,512,128]{3,2,1,0:T(8,128)S(1)}, f32[2,4,512,128]{3,2,1,0:T(8,128)}, u32[]{:S(2)}) copy-start(f32[2,4,512,128]{3,2,1,0:T(8,128)} %get-tuple-element.179) | copy-start | bytes 6291460 | tf_op jit(solution)/shard_map/while
  37.8 1.4 copy-start.1
  39.1 9.2 %collective-permute-start.1 = (bf16[512,256]{0,1:T(8,128)(2,1)S(1)}, bf16[512,256]{0,1:T(8,128)(2,1)S(1)}, u32[]{:S(2)}, u32[]{:S(2)}) collective-permute-start(bf16[512,256]{0,1:T(8,128)(2,1)S(1)} %get-tuple-element.180), channel_id=1, source_target_pairs={{0,4},{4,8},{8,12},{12,16},{16,20},{20,24},{24,28},{1,5},{5,9},{9,... | collective-permute-start | bytes 786440 | tf_op jit(solution)/shard_map/while/body/eval_jaxpr/ppermute | solution.py:12
  42.6 5.5 %collective-permute-start = (s32[512]{0:T(512)S(1)}, s32[512]{0:T(512)S(1)}, u32[]{:S(2)}, u32[]{:S(2)}) collective-permute-start(s32[512]{0:T(512)S(1)} %get-tuple-element.182), channel_id=1, source_target_pairs={{0,4},{4,8},{8,12},{12,16},{16,20},{20,24},{24,28},{1,5},{5,9},{9,... | collective-permute-start | bytes 6152 | tf_op jit(solution)/shard_map/while/body/eval_jaxpr/ppermute | solution.py:12
  46.2 6.0 %collective-permute-start.2 = (bf16[512,256]{0,1:T(8,128)(2,1)S(1)}, bf16[512,256]{0,1:T(8,128)(2,1)S(1)}, u32[]{:S(2)}, u32[]{:S(2)}) collective-permute-start(bf16[512,256]{0,1:T(8,128)(2,1)S(1)} %get-tuple-element.181), channel_id=1, source_target_pairs={{0,4},{4,8},{8,12},{12,16},{16,20},{20,24},{24,28},{1,5},{5,9},{9,... | collective-permute-start | bytes 786440 | tf_op jit(solution)/shard_map/while/body/eval_jaxpr/ppermute | solution.py:12
  48.4 3.9 %copy-start = (f32[2,4,512,128]{3,2,1,0:T(8,128)S(1)}, f32[2,4,512,128]{3,2,1,0:T(8,128)}, u32[]{:S(2)}) copy-start(f32[2,4,512,128]{3,2,1,0:T(8,128)} %get-tuple-element.179) | copy-start | bytes 6291460 | tf_op jit(solution)/shard_map/while
  55.6 1.4 copy-start.1
Sparse Core Ops, SparseCore 0:
  60.3 83.5 all-gather.1
where the time goes:
time: 161 us
  waiting for transfers between devices  83.8 us (52%)
  matrix products  26.4 us (16%)
  starting transfers between devices  17.8 us (11%)
  between operations  13.5 us (8%)
  local copies, waits for them, and re-layouts  11.7 us (7%)
  other arithmetic  7.42 us (5%)
    all_gather x1, waiting for transfers between devices, shards(): lax.all_gather(attended, 'head', axis=1, tiled=True)  83.7 us
    ppermute x6, starting transfers between devices, shifted(): return lax.ppermute(shard, axis, pairs)  17.8 us
    dot_general x3, matrix products, attend(): jnp.einsum('kgts,skd->kgtd', weights.astype(jnp.bfloat16), valued_rows, p...  10.7 us
    dot_general x1, matrix products, shards(): jnp.dot(lax.all_gather(attended, 'head', axis=1, tiled=True), out_weight,...  10.1 us
    dot_general x3, matrix products, attend(): jnp.einsum('tkgd,skd->kgts', grouped_queries, keyed_rows, preferred_eleme...  5.65 us
    reduce_sum x3, other arithmetic, attend(): run_total = run_total * factor + jnp.sum(weights, axis=-1)  5.23 us
    while x4, local copies, waits for them, and re-layouts, shards(): lax.fori_loop(0, reach_shards, turn_step, (softmax_state, (keys, values,...  4.76 us
  transfers between devices with their start and end apart: 7, of which 1 were waited for; matrix products, arithmetic and copies ran while one was open for 5% of the time, Pallas kernels for 0%

commit v1 on v0

--- a/solution.py
+++ b/solution.py
@@ -4,6 +4,19 @@
 from jax.sharding import PartitionSpec as P
 
 HEAD_SIZE = 128
+
+
+def gather_around(value, axis, dim):
+    ways = lax.axis_size(axis)
+    up = [(d, (d + 1) % ways) for d in range(ways)]
+    down = [(d, (d - 1) % ways) for d in range(ways)]
+    earlier, later = ([value], [value])
+    for _ in range(ways // 2):
+        earlier.append(lax.ppermute(earlier[-1], axis, up))
+    for _ in range((ways - 1) // 2):
+        later.append(lax.ppermute(later[-1], axis, down))
+    line = jnp.concatenate([*earlier[::-1], *later[1:]], axis=dim)
+    return jnp.roll(line, (lax.axis_index(axis) - ways // 2) * value.shape[dim], axis=dim)
 
 
 def shifted(shard, axis, by):
@@ -80,9 +93,7 @@
         .astype(jnp.bfloat16)
     )
     mixed = jnp.dot(
-        lax.all_gather(attended, "head", axis=1, tiled=True),
-        out_weight,
-        preferred_element_type=jnp.float32,
+        gather_around(attended, "head", 1), out_weight, preferred_element_type=jnp.float32
     )
     return mixed.astype(jnp.bfloat16)
 

time: 161 us -> 136 us (0.84)
  waiting for transfers between devices: 83.8 us -> 67.5 us
  between operations: 13.5 us -> 0.16 us
  starting transfers between devices: 17.8 us -> 23.2 us
  local copies, waits for them, and re-layouts: 11.7 us -> 16.4 us
  matrix products: 26.4 us -> 21.8 us
    all_gather x1 -> x0, waiting for transfers between devices: 83.7 us -> none  [shards(): lax.all_gather(attended, 'head', axis=1, tiled=True)]
    ppermute x0 -> x3, waiting for transfers between devices: none -> 67.5 us  [the longest x2 48.5 us: gather_around(): earlier.append(lax.ppermute(earlier[-1], axis, up))]
    ppermute x0 -> x3, starting transfers between devices: none -> 5.44 us  [the longest x1 3.82 us: gather_around(): later.append(lax.ppermute(later[-1], axis, down))]
    dot_general x1, matrix products: 10.1 us -> 5.48 us  [shards(): jnp.dot(gather_around(attended, 'head', 1), out_weight, preferred_element...]
    unnamed x2 -> x15, local copies, waits for them, and re-layouts: 1.5 us -> 5.4 us
  transfers between devices with their start and end apart: 7 -> 9, of which waited for: 1 -> 3; matrix products, arithmetic and copies ran while one was open for 5% -> 7% of each run, Pallas kernels for 0% -> 0%
where the time goes in v1:
time: 136 us
  waiting for transfers between devices  67.5 us (50%)
  starting transfers between devices  23.2 us (17%)
  matrix products  21.8 us (16%)
  local copies, waits for them, and re-layouts  16.4 us (12%)
  other arithmetic  6.46 us (5%)
    ppermute x2, waiting for transfers between devices, gather_around(): earlier.append(lax.ppermute(earlier[-1], axis, up))  48.5 us
    ppermute x1, waiting for transfers between devices, gather_around(): later.append(lax.ppermute(later[-1], axis, down))  19 us
    ppermute x6, starting transfers between devices, shifted(): return lax.ppermute(shard, axis, pairs)  17.8 us
    dot_general x3, matrix products, attend(): jnp.einsum('kgts,skd->kgtd', weights.astype(jnp.bfloat16), valued_rows, p...  10.7 us
    dot_general x3, matrix products, attend(): jnp.einsum('tkgd,skd->kgts', grouped_queries, keyed_rows, preferred_eleme...  5.65 us
    dot_general x1, matrix products, shards(): jnp.dot(gather_around(attended, 'head', 1), out_weight, preferred_element...  5.48 us
    unnamed x15, local copies, waits for them, and re-layouts  5.4 us
    reduce_sum x3, other arithmetic, attend(): run_total = run_total * factor + jnp.sum(weights, axis=-1)  5.23 us
  transfers between devices with their start and end apart: 9, of which 3 were waited for; matrix products, arithmetic and copies ran while one was open for 7% of the time, Pallas kernels for 0%

profile of v1, /device:TPU:0, one launch (start us, length us, event | category | flops | bytes accessed | tf_op | source)
XLA Modules:
  0.0 135.8 jit_solution(2024542411239677136)
XLA Ops:
  1.2 1.1 copy.33
  2.3 1.0 reshape.65
  3.3 1.1 copy.34
  4.4 1.7 %reshape.67 = bf16[512,2,128]{2,1,0:T(2,128)(2,1)} reshape(bf16[512,256]{1,0:T(8,128)(2,1)} %param.9) | data formatting | bytes 524288 | tf_op jit(solution)/shard_map/reshape | solution.py:37
  6.1 1.5 %copy.28 = bf16[512,1024]{0,1:T(8,128)(2,1)S(1)} copy(bf16[512,1024]{1,0:T(8,128)(2,1)} %param.7) | data formatting | bytes 2097152 | tf_op args[0]
  8.3 1.6 %fusion.12 = (f32[2,4,512]{2,1,0:T(4,128)S(1)}, f32[2,512,512,4]{2,1,3,0:T(8,128)S(1)}) fusion(pred[512,512]{0,1:T(8,128)(4,1)S(1)} %fusion.24, bf16[512,2,4,128]{0,3,2,1:T(8,128)(2,1)S(1)} %bitcast.84, bf16[512,2,128,1]{2,1,0,3:T(2,128)(2,1)S(1)} %bitcast.89), kind=kOutput, calls=%fused_computation.17 | convolution fusion | flops 543158272 | bytes 9977856 | tf_op jit(solution)/shard_map/tkgd,skd->kgts/dot_general | solution.py:38
  9.9 1.7 %fusion.11 = f32[2,4,512]{2,1,0:T(4,128)S(1)} fusion(f32[2,512,512,4]{2,1,3,0:T(8,128)S(1)} %get-tuple-element.98, f32[2,4,512]{2,1,0:T(4,128)S(1)} %broadcast_maximum_fusion, pred[512,512]{0,1:T(8,128)(4,1)S(1)} %fusion.24), kind=kLoop, calls=%fused_computation.16 | loop fusion | flops 8384512 | bytes 8683520 | tf_op jit(solution)/shard_map/reduce_sum | solution.py:49
  11.7 3.9 %fusion.18 = f32[2,4,512,128]{3,2,1,0:T(8,128)} fusion(f32[2,512,512,4]{2,1,3,0:T(8,128)S(1)} %get-tuple-element.98, f32[2,4,512]{2,1,0:T(4,128)S(1)} %broadcast_maximum_fusion, pred[512,512]{0,1:T(8,128)(4,1)S(1)} %fusion.24, f32[2,4,512]{2,1,0:T(4,128)S(1)} %get-tuple-element.95, bf16[512,2,128,1]{2,1,0,3:T(2,128)(2,1)S(1)} %bitcast.93), kind=kOutput, calls=%fused_computation.23 | convolution fusion | flops 545783808 | bytes 11042816 | tf_op jit(solution)/shard_map/kgts,skd->kgtd/dot_general | solution.py:50
  15.6 35.6 %while.20 = (s32[]{:T(128)}, f32[2,4,512]{2,1,0:T(4,128)S(1)}, f32[2,4,512]{2,1,0:T(4,128)S(1)}, f32[2,4,512,128]{3,2,1,0:T(8,128)}, bf16[512,256]{0,1:T(8,128)(...) while((s32[]{:T(128)}, f32[2,4,512]{2,1,0:T(4,128)S(1)}, ...), condition=%wide.region_7.8_spmd, body=%wide.region_4.7_spmd.sunk | while | flops 1098129408 | bytes 52183316 | solution.py:85
  15.6 2.4 %collective-permute-start.1 = (bf16[512,256]{0,1:T(8,128)(2,1)S(1)}, bf16[512,256]{0,1:T(8,128)(2,1)S(1)}, u32[]{:S(2)}, u32[]{:S(2)}) collective-permute-start(bf16[512,256]{0,1:T(8,128)(2,1)S(1)} %get-tuple-element.180), channel_id=1, source_target_pairs={{0,4},{4,8},{8,12},{12,16},{16,20},{20,24},{24,28},{1,5},{5,9},{9,... | collective-permute-start | bytes 786440 | tf_op jit(solution)/shard_map/while/body/eval_jaxpr/ppermute | solution.py:25
  18.0 4.5 %collective-permute-start = (s32[512]{0:T(512)S(1)}, s32[512]{0:T(512)S(1)}, u32[]{:S(2)}, u32[]{:S(2)}) collective-permute-start(s32[512]{0:T(512)S(1)} %get-tuple-element.182), channel_id=1, source_target_pairs={{0,4},{4,8},{8,12},{12,16},{16,20},{20,24},{24,28},{1,5},{5,9},{9,... | collective-permute-start | bytes 6152 | tf_op jit(solution)/shard_map/while/body/eval_jaxpr/ppermute | solution.py:25
  22.5 1.9 %collective-permute-start.2 = (bf16[512,256]{0,1:T(8,128)(2,1)S(1)}, bf16[512,256]{0,1:T(8,128)(2,1)S(1)}, u32[]{:S(2)}, u32[]{:S(2)}) collective-permute-start(bf16[512,256]{0,1:T(8,128)(2,1)S(1)} %get-tuple-element.181), channel_id=1, source_target_pairs={{0,4},{4,8},{8,12},{12,16},{16,20},{20,24},{24,28},{1,5},{5,9},{9,... | collective-permute-start | bytes 786440 | tf_op jit(solution)/shard_map/while/body/eval_jaxpr/ppermute | solution.py:25
  24.7 2.0 %fusion.47 = (f32[2,4,512]{2,1,0:T(4,128)S(1)}, f32[2,512,512,4]{2,1,3,0:T(8,128)S(1)}) fusion(pred[512,512]{0,1:T(8,128)(4,1)S(1)} %broadcast_compare_fusion.2, bf16[512,2,128,1]{0,2,3,1:T(8,128)(2,1)S(1)} %bitcast.78, bf16[512,2,4,128]{3,0,2,1:T(8,128)(2,1)S(1)} %get-tuple-element.194), kind=kOutput, calls=%fused_computation.4.clone.1 | convolution fusion | flops 543158272 | bytes 9977856 | tf_op jit(solution)/shard_map/while/body/eval_jaxpr/tkgd,skd->kgts/dot_general | solution.py:38
  26.7 1.7 %fusion.48 = f32[2,4,512]{2,1,0:T(4,128)S(1)} fusion(f32[2,512,512,4]{2,1,3,0:T(8,128)S(1)} %get-tuple-element.163, f32[2,4,512]{2,1,0:T(4,128)S(1)} %max.4, pred[512,512]{0,1:T(8,128)(4,1)S(1)} %broadcast_compare_fusion.2), kind=kLoop, calls=%fused_computation.3.clone.1 | loop fusion | flops 8384512 | bytes 8683520 | tf_op jit(solution)/shard_map/while/body/eval_jaxpr/reduce_sum | solution.py:49
  28.5 3.4 %multiply_add_fusion.5 = f32[2,4,512,128]{3,2,1,0:T(8,128)S(1)} fusion(f32[2,4,512,128]{3,2,1,0:T(8,128)S(1)} %copy-done, bf16[512,2,128,1]{0,2,3,1:T(8,128)(2,1)S(1)} %bitcast.86, f32[2,512,512,4]{2,1,3,0:T(8,128)S(1)} %get-tuple-element.163, f32[2,4,512]{2,1,0:T(4,128)S(1)} %max.4, pred[512,512]{0,1:T(8,128)(4,1)S(1)} %broadcast_compare_fusion.2, ...), kind=kOutput, calls=%fused_computation.7.clone.1 | convolution fusion | flops 546308096 | bytes 13139968 | tf_op jit(solution)/shard_map/while/body/eval_jaxpr/kgts,skd->kgtd/dot_general | solution.py:50
  32.0 1.3 copy-done.1
  33.3 3.5 %collective-permute-start.1 = (bf16[512,256]{0,1:T(8,128)(2,1)S(1)}, bf16[512,256]{0,1:T(8,128)(2,1)S(1)}, u32[]{:S(2)}, u32[]{:S(2)}) collective-permute-start(bf16[512,256]{0,1:T(8,128)(2,1)S(1)} %get-tuple-element.180), channel_id=1, source_target_pairs={{0,4},{4,8},{8,12},{12,16},{16,20},{20,24},{24,28},{1,5},{5,9},{9,... | collective-permute-start | bytes 786440 | tf_op jit(solution)/shard_map/while/body/eval_jaxpr/ppermute | solution.py:25
  36.8 3.5 %collective-permute-start = (s32[512]{0:T(512)S(1)}, s32[512]{0:T(512)S(1)}, u32[]{:S(2)}, u32[]{:S(2)}) collective-permute-start(s32[512]{0:T(512)S(1)} %get-tuple-element.182), channel_id=1, source_target_pairs={{0,4},{4,8},{8,12},{12,16},{16,20},{20,24},{24,28},{1,5},{5,9},{9,... | collective-permute-start | bytes 6152 | tf_op jit(solution)/shard_map/while/body/eval_jaxpr/ppermute | solution.py:25
  40.3 1.9 %collective-permute-start.2 = (bf16[512,256]{0,1:T(8,128)(2,1)S(1)}, bf16[512,256]{0,1:T(8,128)(2,1)S(1)}, u32[]{:S(2)}, u32[]{:S(2)}) collective-permute-start(bf16[512,256]{0,1:T(8,128)(2,1)S(1)} %get-tuple-element.181), channel_id=1, source_target_pairs={{0,4},{4,8},{8,12},{12,16},{16,20},{20,24},{24,28},{1,5},{5,9},{9,... | collective-permute-start | bytes 786440 | tf_op jit(solution)/shard_map/while/body/eval_jaxpr/ppermute | solution.py:25
  42.5 2.0 %fusion.47 = (f32[2,4,512]{2,1,0:T(4,128)S(1)}, f32[2,512,512,4]{2,1,3,0:T(8,128)S(1)}) fusion(pred[512,512]{0,1:T(8,128)(4,1)S(1)} %broadcast_compare_fusion.2, bf16[512,2,128,1]{0,2,3,1:T(8,128)(2,1)S(1)} %bitcast.78, bf16[512,2,4,128]{3,0,2,1:T(8,128)(2,1)S(1)} %get-tuple-element.194), kind=kOutput, calls=%fused_computation.4.clone.1 | convolution fusion | flops 543158272 | bytes 9977856 | tf_op jit(solution)/shard_map/while/body/eval_jaxpr/tkgd,skd->kgts/dot_general | solution.py:38
  44.6 1.7 %fusion.48 = f32[2,4,512]{2,1,0:T(4,128)S(1)} fusion(f32[2,512,512,4]{2,1,3,0:T(8,128)S(1)} %get-tuple-element.163, f32[2,4,512]{2,1,0:T(4,128)S(1)} %max.4, pred[512,512]{0,1:T(8,128)(4,1)S(1)} %broadcast_compare_fusion.2), kind=kLoop, calls=%fused_computation.3.clone.1 | loop fusion | flops 8384512 | bytes 8683520 | tf_op jit(solution)/shard_map/while/body/eval_jaxpr/reduce_sum | solution.py:49
  46.4 3.4 %multiply_add_fusion.5 = f32[2,4,512,128]{3,2,1,0:T(8,128)S(1)} fusion(f32[2,4,512,128]{3,2,1,0:T(8,128)S(1)} %copy-done, bf16[512,2,128,1]{0,2,3,1:T(8,128)(2,1)S(1)} %bitcast.86, f32[2,512,512,4]{2,1,3,0:T(8,128)S(1)} %get-tuple-element.163, f32[2,4,512]{2,1,0:T(4,128)S(1)} %max.4, pred[512,512]{0,1:T(8,128)(4,1)S(1)} %broadcast_compare_fusion.2, ...), kind=kOutput, calls=%fused_computation.7.clone.1 | convolution fusion | flops 546308096 | bytes 13139968 | tf_op jit(solution)/shard_map/while/body/eval_jaxpr/kgts,skd->kgtd/dot_general | solution.py:50
  49.9 1.3 copy-done.1
  51.2 1.9 %copy.36 = f32[2,4,512,128]{2,3,1,0:T(8,128)S(1)} copy(f32[2,4,512,128]{3,2,1,0:T(8,128)} %get-tuple-element.53) | data formatting | bytes 4194304 | tf_op jit(solution)/shard_map/while | solution.py:85
  53.4 1.6 %collective-permute-start.3 = (bf16[512,1024]{0,1:T(8,128)(2,1)S(1)}, bf16[512,1024]{0,1:T(8,128)(2,1)S(1)}, u32[]{:S(2)}, u32[]{:S(2)}) collective-permute-start(bf16[512,1024]{0,1:T(8,128)(2,1)S(1)} %bitcast.79), channel_id=1, source_target_pairs={{0,1},{1,2},{2,3},{3,0},{4,5},{5,6},{6,7},{7,4},{8,9},{9,10},{10,1... | collective-permute-start | bytes 3145736 | tf_op jit(solution)/shard_map/ppermute | solution.py:15
  55.0 24.7 %collective-permute-done.3 = bf16[512,1024]{0,1:T(8,128)(2,1)S(1)} collective-permute-done((bf16[512,1024]{0,1:T(8,128)(2,1)S(1)}, bf16[512,1024]{0,1:T(8,128)(2,1)S(1)}, u32[]{:S(2)}, u32[]{:S(2)}) %collective-permute-start.3) | collective-permute-done | bytes 1048608 | tf_op jit(solution)/shard_map/ppermute | solution.py:15
  79.7 3.8 %collective-permute-start.5 = (bf16[512,1024]{0,1:T(8,128)(2,1)S(1)}, bf16[512,1024]{0,1:T(8,128)(2,1)S(1)}, u32[]{:S(2)}, u32[]{:S(2)}) collective-permute-start(bf16[512,1024]{0,1:T(8,128)(2,1)S(1)} %bitcast.80), channel_id=1, source_target_pairs={{0,3},{1,0},{2,1},{3,2},{4,7},{5,4},{6,5},{7,6},{8,11},{9,8},{10,9... | collective-permute-start | bytes 3145736 | tf_op jit(solution)/shard_map/ppermute | solution.py:17
  83.5 23.8 %collective-permute-done.4 = bf16[512,1024]{0,1:T(8,128)(2,1)} collective-permute-done((bf16[512,1024]{0,1:T(8,128)(2,1)S(1)}, bf16[512,1024]{0,1:T(8,128)(2,1)}, u32[]{:S(2)}, u32[]{:S(2)}) %collective-permute-start.4) | collective-permute-done | bytes 1048608 | tf_op jit(solution)/shard_map/ppermute | solution.py:15
  107.3 1.3 constant_dynamic-update-slice_fusion.7
  108.8 19.0 %collective-permute-done.5 = bf16[512,1024]{0,1:T(8,128)(2,1)S(1)} collective-permute-done((bf16[512,1024]{0,1:T(8,128)(2,1)S(1)}, bf16[512,1024]{0,1:T(8,128)(2,1)S(1)}, u32[]{:S(2)}, u32[]{:S(2)}) %collective-permute-start.5) | collective-permute-done | bytes 1048608 | tf_op jit(solution)/shard_map/ppermute | solution.py:17
  127.9 1.4 %constant_dynamic-update-slice_fusion.3 = bf16[512,8192]{0,1:T(8,128)(2,1)S(1)} fusion(bf16[512,8192]{0,1:T(8,128)(2,1)S(1)} %constant_dynamic-update-slice_fusion.4, bf16[512,1024]{0,1:T(8,128)(2,1)} %collective-permute-done.4), kind=kLoop, calls=%fused_computation.34 | loop fusion | bytes 2097152
  130.4 5.5 %fusion.21 = bf16[512,1024]{1,0:T(8,128)(2,1)} fusion(bf16[4096,1024]{1,0:T(8,128)(2,1)S(1)} %bitcast.96, bf16[512,8192]{0,1:T(8,128)(2,1)S(1)} %constant_dynamic-update-slice_fusion, s32[]{:T(128)S(6)} %select_n.24), kind=kOutput, calls=%fused_computation.24 | convolution fusion | flops 4295491584 | bytes 13631492 | tf_op jit(solution)/shard_map/dot_general | solution.py:95
  (52 shorter events, 4.0 us)
Async XLA Ops:
  8.3 3.4 %copy-start.2 = (bf16[512,2,128]{2,1,0:T(2,128)(2,1)S(1)}, bf16[512,2,128]{2,1,0:T(2,128)(2,1)}, u32[]{:S(2)}) copy-start(bf16[512,2,128]{2,1,0:T(2,128)(2,1)} %reshape.67) | copy-start | bytes 786436
  15.6 9.1 %collective-permute-start.1 = (bf16[512,256]{0,1:T(8,128)(2,1)S(1)}, bf16[512,256]{0,1:T(8,128)(2,1)S(1)}, u32[]{:S(2)}, u32[]{:S(2)}) collective-permute-start(bf16[512,256]{0,1:T(8,128)(2,1)S(1)} %get-tuple-element.180), channel_id=1, source_target_pairs={{0,4},{4,8},{8,12},{12,16},{16,20},{20,24},{24,28},{1,5},{5,9},{9,... | collective-permute-start | bytes 786440 | tf_op jit(solution)/shard_map/while/body/eval_jaxpr/ppermute | solution.py:25
  18.0 6.4 %collective-permute-start = (s32[512]{0:T(512)S(1)}, s32[512]{0:T(512)S(1)}, u32[]{:S(2)}, u32[]{:S(2)}) collective-permute-start(s32[512]{0:T(512)S(1)} %get-tuple-element.182), channel_id=1, source_target_pairs={{0,4},{4,8},{8,12},{12,16},{16,20},{20,24},{24,28},{1,5},{5,9},{9,... | collective-permute-start | bytes 6152 | tf_op jit(solution)/shard_map/while/body/eval_jaxpr/ppermute | solution.py:25
  22.5 6.0 %collective-permute-start.2 = (bf16[512,256]{0,1:T(8,128)(2,1)S(1)}, bf16[512,256]{0,1:T(8,128)(2,1)S(1)}, u32[]{:S(2)}, u32[]{:S(2)}) collective-permute-start(bf16[512,256]{0,1:T(8,128)(2,1)S(1)} %get-tuple-element.181), channel_id=1, source_target_pairs={{0,4},{4,8},{8,12},{12,16},{16,20},{20,24},{24,28},{1,5},{5,9},{9,... | collective-permute-start | bytes 786440 | tf_op jit(solution)/shard_map/while/body/eval_jaxpr/ppermute | solution.py:25
  24.7 3.9 %copy-start = (f32[2,4,512,128]{3,2,1,0:T(8,128)S(1)}, f32[2,4,512,128]{3,2,1,0:T(8,128)}, u32[]{:S(2)}) copy-start(f32[2,4,512,128]{3,2,1,0:T(8,128)} %get-tuple-element.179) | copy-start | bytes 6291460 | tf_op jit(solution)/shard_map/while
  31.9 1.4 copy-start.1
  33.3 9.2 %collective-permute-start.1 = (bf16[512,256]{0,1:T(8,128)(2,1)S(1)}, bf16[512,256]{0,1:T(8,128)(2,1)S(1)}, u32[]{:S(2)}, u32[]{:S(2)}) collective-permute-start(bf16[512,256]{0,1:T(8,128)(2,1)S(1)} %get-tuple-element.180), channel_id=1, source_target_pairs={{0,4},{4,8},{8,12},{12,16},{16,20},{20,24},{24,28},{1,5},{5,9},{9,... | collective-permute-start | bytes 786440 | tf_op jit(solution)/shard_map/while/body/eval_jaxpr/ppermute | solution.py:25
  36.8 5.5 %collective-permute-start = (s32[512]{0:T(512)S(1)}, s32[512]{0:T(512)S(1)}, u32[]{:S(2)}, u32[]{:S(2)}) collective-permute-start(s32[512]{0:T(512)S(1)} %get-tuple-element.182), channel_id=1, source_target_pairs={{0,4},{4,8},{8,12},{12,16},{16,20},{20,24},{24,28},{1,5},{5,9},{9,... | collective-permute-start | bytes 6152 | tf_op jit(solution)/shard_map/while/body/eval_jaxpr/ppermute | solution.py:25
  40.3 6.0 %collective-permute-start.2 = (bf16[512,256]{0,1:T(8,128)(2,1)S(1)}, bf16[512,256]{0,1:T(8,128)(2,1)S(1)}, u32[]{:S(2)}, u32[]{:S(2)}) collective-permute-start(bf16[512,256]{0,1:T(8,128)(2,1)S(1)} %get-tuple-element.181), channel_id=1, source_target_pairs={{0,4},{4,8},{8,12},{12,16},{16,20},{20,24},{24,28},{1,5},{5,9},{9,... | collective-permute-start | bytes 786440 | tf_op jit(solution)/shard_map/while/body/eval_jaxpr/ppermute | solution.py:25
  42.5 3.9 %copy-start = (f32[2,4,512,128]{3,2,1,0:T(8,128)S(1)}, f32[2,4,512,128]{3,2,1,0:T(8,128)}, u32[]{:S(2)}) copy-start(f32[2,4,512,128]{3,2,1,0:T(8,128)} %get-tuple-element.179) | copy-start | bytes 6291460 | tf_op jit(solution)/shard_map/while
  49.8 1.4 copy-start.1
  53.4 26.3 %collective-permute-start.3 = (bf16[512,1024]{0,1:T(8,128)(2,1)S(1)}, bf16[512,1024]{0,1:T(8,128)(2,1)S(1)}, u32[]{:S(2)}, u32[]{:S(2)}) collective-permute-start(bf16[512,1024]{0,1:T(8,128)(2,1)S(1)} %bitcast.79), channel_id=1, source_target_pairs={{0,1},{1,2},{2,3},{3,0},{4,5},{5,6},{6,7},{7,4},{8,9},{9,10},{10,1... | collective-permute-start | bytes 3145736 | tf_op jit(solution)/shard_map/ppermute | solution.py:15
  79.7 27.6 %collective-permute-start.4 = (bf16[512,1024]{0,1:T(8,128)(2,1)S(1)}, bf16[512,1024]{0,1:T(8,128)(2,1)}, u32[]{:S(2)}, u32[]{:S(2)}) collective-permute-start(bf16[512,1024]{0,1:T(8,128)(2,1)S(1)} %collective-permute-done.3), channel_id=1, source_target_pairs={{0,1},{1,2},{2,3},{3,0},{4,5},{5,6},{6,7},{7,4},{8,9},{9,10},{10,1... | collective-permute-start | bytes 3145736 | tf_op jit(solution)/shard_map/ppermute | solution.py:15
  79.7 48.1 %collective-permute-start.5 = (bf16[512,1024]{0,1:T(8,128)(2,1)S(1)}, bf16[512,1024]{0,1:T(8,128)(2,1)S(1)}, u32[]{:S(2)}, u32[]{:S(2)}) collective-permute-start(bf16[512,1024]{0,1:T(8,128)(2,1)S(1)} %bitcast.80), channel_id=1, source_target_pairs={{0,3},{1,0},{2,1},{3,2},{4,7},{5,4},{6,5},{7,6},{8,11},{9,8},{10,9... | collective-permute-start | bytes 3145736 | tf_op jit(solution)/shard_map/ppermute | solution.py:17
  83.5 46.0 %slice-start = ((s8[8388608]{0:T(1024)(128)(4,1)}), s8[4194304]{0:T(1024)(128)(4,1)S(1)}, s32[]{:S(2)}) async-start(s8[8388608]{0:T(1024)(128)(4,1)} %bitcast.95), calls=%async_computation | async-start | bytes 8388608
  127.9 2.5 %slice-start.1 = ((s8[8388608]{0:T(1024)(128)(4,1)}), s8[4194304]{0:T(1024)(128)(4,1)S(1)}, s32[]{:S(2)}) async-start(s8[8388608]{0:T(1024)(128)(4,1)} %bitcast.95), calls=%async_computation.1 | async-start | bytes 8388608
